TPU v7x, 32 devices: a whole 2x2x4 slice. The times are simulated.
32 devices in a mesh: seq: 8 (over z, y), mp: 4 (over x, core).
Axes of the slice: x: 2, y: 2, z: 4, core: 2. Of those that a mesh axis runs over, the one named last changes fastest.
Arguments:
- tokens: bfloat16 [4096, 768], P('seq'), may hold values from -6 to 6
- item_lengths: int32 [8], replicated, may hold values from 1 to 2048, 4096 in all
- w_qkv: bfloat16 [3, 768, 768], P(None, None, 'mp'), may hold values from -2 to 2
- b_qv: float32 [2, 768], P(None, 'mp'), may hold values from -2 to 2
- taps: float32 [12, 33], P('mp'), may hold values from -0.072 to 0.072
- w_out: bfloat16 [768, 768], P('mp'), may hold values from -1.75 to 1.75
- b_out: float32 [768], replicated, may hold values from -3 to 3
- ln1_gain: float32 [768], replicated, may hold values from 0.5 to 1.5
- ln1_bias: float32 [768], replicated, may hold values from -2 to 2
- w_up: bfloat16 [768, 3072], P(None, 'mp'), may hold values from -0.21875 to 0.21875
- b_up: float32 [3072], P('mp'), may hold values from -3 to 3
- w_down: bfloat16 [3072, 768], P('mp'), may hold values from -0.109375 to 0.109375
- b_down: float32 [768], replicated, may hold values from -3 to 3
- ln2_gain: float32 [768], replicated, may hold values from 0.5 to 1.5
- ln2_bias: float32 [768], replicated, may hold values from -2 to 2
- d_out: bfloat16 [4096, 768], P('seq'), may hold values from -6 to 6
Outputs:
- layer_output: bfloat16 [4096, 768], P('seq')
- d_tokens: bfloat16 [4096, 768], P('seq')
- d_w_qkv: float32 [3, 768, 768], P(None, None, 'mp')
- d_b_qv: float32 [2, 768], P(None, 'mp')
- d_taps: float32 [12, 33], P('mp')
- d_w_out: float32 [768, 768], P('mp')
- d_b_out: float32 [768], replicated
- d_ln1_gain: float32 [768], replicated
- d_ln1_bias: float32 [768], replicated
- d_w_up: float32 [768, 3072], P(None, 'mp')
- d_b_up: float32 [3072], P('mp')
- d_w_down: float32 [3072, 768], P('mp')
- d_b_down: float32 [768], replicated
- d_ln2_gain: float32 [768], replicated
- d_ln2_bias: float32 [768], replicated
Inputs may be any that keep to these rules, and one draw needn't show every extreme that they name: `item_lengths`: the lengths sum to 4096; the largest is exactly 2048, and no item is longer than 4096.
All inputs are finite; a program needn't handle non-finite values.
Results may differ from a plain program's by a relative error of at most 0.017.
Values may be sent and summed in bfloat16 or wider, within the bound.
No kernel may reach another device: no remote copies, remote signals or barrier semaphores. Data moves between devices by JAX's collectives and lax.ppermute only.
A program may use at most 192 MiB of HBM per device.

v0:
```python
import math
import jax
import jax.numpy as jnp
from jax import lax
from jax.sharding import PartitionSpec as P

SHRINK = 0.95
NORM_EPS = 1e-06
LAYER_EPS = 1e-05


def padded(cells, sides, width):
    for axis, dim in sides:
        count = lax.axis_size(axis)
        ends = count - 1
        head = lax.slice_in_dim(cells, 0, width, axis=dim)
        tail = lax.slice_in_dim(cells, cells.shape[dim] - width, cells.shape[dim], axis=dim)
        cells = jnp.concatenate(
            [
                lax.ppermute(tail, axis, [(i, (i + 1) % count) for i in range(ends)]),
                cells,
                lax.ppermute(head, axis, [((i + 1) % count, i) for i in range(ends)]),
            ],
            axis=dim,
        )
    return cells


def item_index(positions, ends):
    inside = (positions >= 0) & (positions < ends[-1])
    counted = jnp.sum((positions[:, None] >= ends[None, :]).astype(jnp.int32), axis=1)
    return jnp.where(inside, counted, -1)


def layer_norm(hidden, gain, shift):
    center = hidden - jnp.mean(hidden, axis=-1, keepdims=True)
    scale = lax.rsqrt(jnp.mean(center * center, axis=-1, keepdims=True) + LAYER_EPS)
    normed = center * scale
    return (normed * gain + shift, normed, scale)


def layer_norm_back(grad, normed, scale, gain):
    d_gain = jnp.sum(grad * normed, axis=0)
    d_shift = jnp.sum(grad, axis=0)
    d_normed = grad * gain
    centered = d_normed - jnp.mean(d_normed, axis=-1, keepdims=True)
    d_hidden = scale * (centered - normed * jnp.mean(d_normed * normed, axis=-1, keepdims=True))
    return (d_hidden, d_gain, d_shift)


def block_rows(row_count):
    bound = min(row_count, 1024)
    return max((candidate for candidate in range(1, bound + 1) if row_count % candidate == 0))


def fold_blocks(carry, arrays, start, work):
    row_count = arrays[0].shape[0]
    width = block_rows(row_count)
    stacked = tuple(
        (array.reshape((row_count // width, width) + array.shape[1:]) for array in arrays)
    )
    offsets = start + width * jnp.arange(row_count // width, dtype=jnp.int32)

    def advance(state, inputs):
        return (work(state, inputs[:-1], inputs[-1]), None)

    result, _ = lax.scan(advance, carry, stacked + (offsets,))
    return result


def collision_back(queries, keys_heads, values_heads, d_attn_heads, same):
    scores = jnp.einsum("bhe,khe->hbk", queries, keys_heads, preferred_element_type=jnp.float32)
    cosine = SHRINK * scores
    closeness = 1.0 - jnp.arccos(cosine) / math.pi
    weights = (same[None] * closeness**8).astype(jnp.bfloat16)
    d_weights = jnp.einsum(
        "bhe,khe->hbk", d_attn_heads, values_heads, preferred_element_type=jnp.float32
    )
    slope = same[None] * 8.0 * closeness**7 * SHRINK / (math.pi * jnp.sqrt(1.0 - cosine * cosine))
    d_scores = (d_weights * slope).astype(jnp.bfloat16)
    return (weights, d_scores)


def per_device(
    tokens,
    item_lengths,
    w_qkv,
    b_qv,
    taps,
    w_out,
    b_out,
    ln1_gain,
    ln1_bias,
    w_up,
    b_up,
    w_down,
    b_down,
    ln2_gain,
    ln2_bias,
    d_out,
):
    local_rows = tokens.shape[0]
    heads_here = taps.shape[0]
    kernel = taps.shape[1]
    radius = (kernel - 1) // 2
    columns = w_qkv.shape[2]
    head_size = columns // heads_here
    ends = jnp.cumsum(item_lengths)
    first_row = lax.axis_index("seq") * local_rows
    query_items = item_index(first_row + jnp.arange(local_rows, dtype=jnp.int32), ends)
    rim_items = item_index(
        first_row - radius + jnp.arange(local_rows + 2 * radius, dtype=jnp.int32), ends
    )
    tap_columns = jnp.repeat(taps, head_size, axis=0).T
    bias_rows = jnp.stack([b_qv[0], jnp.zeros_like(b_qv[0]), b_qv[1]])
    projected = (
        jnp.einsum("td,ide->ite", tokens, w_qkv, preferred_element_type=jnp.float32)
        + bias_rows[:, None, :]
    )
    query_raw = projected[0].reshape(local_rows, heads_here, head_size)
    key_raw = projected[1].reshape(local_rows, heads_here, head_size)
    query_scale = lax.rsqrt(jnp.sum(query_raw * query_raw, axis=-1, keepdims=True) + NORM_EPS)
    key_scale = lax.rsqrt(jnp.sum(key_raw * key_raw, axis=-1, keepdims=True) + NORM_EPS)
    query_unit = query_raw * query_scale
    key_unit = key_raw * key_scale
    query_low = query_unit.astype(jnp.bfloat16)
    key_low = key_unit.astype(jnp.bfloat16)
    value_low = projected[2].astype(jnp.bfloat16)
    packed = jnp.concatenate([key_low.reshape(local_rows, columns), value_low], axis=1)
    zero_heads = jnp.zeros((local_rows, heads_here, head_size), jnp.float32)

    def split_pair(block):
        count = block.shape[0]
        first = block[:, :columns].reshape(count, heads_here, head_size)
        second = block[:, columns : 2 * columns].reshape(count, heads_here, head_size)
        return (first, second)

    def attend(state, pieces, offset):
        keys_heads, values_heads = split_pair(pieces[0])
        key_items = item_index(offset + jnp.arange(keys_heads.shape[0], dtype=jnp.int32), ends)
        same = (query_items[:, None] == key_items[None, :]).astype(jnp.float32)
        scores = jnp.einsum(
            "bhe,khe->hbk", query_low, keys_heads, preferred_element_type=jnp.float32
        )
        closeness = 1.0 - jnp.arccos(SHRINK * scores) / math.pi
        weights = (same[None] * closeness**8).astype(jnp.bfloat16)
        return state + jnp.einsum(
            "hbk,khe->bhe", weights, values_heads, preferred_element_type=jnp.float32
        )

    attended = fold_blocks(
        zero_heads, (lax.all_gather(packed, "seq", axis=0, tiled=True),), jnp.int32(0), attend
    )
    attn_scale = lax.rsqrt(jnp.sum(attended * attended, axis=-1, keepdims=True) + NORM_EPS)
    attn_unit = attended * attn_scale
    value_rim = padded(value_low, (("seq", 0),), radius).astype(jnp.float32)
    convolved = jnp.zeros((local_rows, columns), jnp.float32)
    same_list = []
    for shift_at in range(kernel):
        same_rows = (rim_items[shift_at : shift_at + local_rows] == query_items).astype(
            jnp.float32
        )[:, None]
        same_list.append(same_rows)
        convolved = (
            convolved
            + tap_columns[shift_at] * same_rows * value_rim[shift_at : shift_at + local_rows]
        )
    context_low = (attn_unit.reshape(local_rows, columns) + convolved).astype(jnp.bfloat16)
    branch = lax.psum(jnp.dot(context_low, w_out, preferred_element_type=jnp.float32), "mp")
    first_sum = tokens.astype(jnp.float32) + branch + b_out
    first_out, normed_one, scale_one = layer_norm(first_sum, ln1_gain, ln1_bias)
    first_low = first_out.astype(jnp.bfloat16)
    inner = jnp.dot(first_low, w_up, preferred_element_type=jnp.float32) + b_up
    act_low = jax.nn.gelu(inner, approximate=False).astype(jnp.bfloat16)
    mixed = lax.psum(jnp.dot(act_low, w_down, preferred_element_type=jnp.float32), "mp")
    second_sum = first_out + mixed + b_down
    result, normed_two, scale_two = layer_norm(second_sum, ln2_gain, ln2_bias)
    layer_output = result.astype(jnp.bfloat16)
    d_second, d_ln2_gain, d_ln2_bias = layer_norm_back(
        d_out.astype(jnp.float32), normed_two, scale_two, ln2_gain
    )
    d_second_low = d_second.astype(jnp.bfloat16)
    d_b_down = jnp.sum(d_second, axis=0)
    d_w_down = jnp.einsum("tf,td->fd", act_low, d_second_low, preferred_element_type=jnp.float32)
    d_act = jnp.einsum("td,fd->tf", d_second_low, w_down, preferred_element_type=jnp.float32)
    normal_cdf = 0.5 * (1.0 + lax.erf(inner / math.sqrt(2.0)))
    normal_pdf = jnp.exp(-0.5 * inner * inner) / math.sqrt(2.0 * math.pi)
    d_inner_low = (d_act * (normal_cdf + inner * normal_pdf)).astype(jnp.bfloat16)
    d_b_up = jnp.sum(d_inner_low.astype(jnp.float32), axis=0)
    d_w_up = jnp.einsum("td,tf->df", first_low, d_inner_low, preferred_element_type=jnp.float32)
    d_first_part = jnp.einsum("tf,df->td", d_inner_low, w_up, preferred_element_type=jnp.float32)
    d_first_out = d_second + lax.psum(d_first_part, "mp")
    d_first, d_ln1_gain, d_ln1_bias = layer_norm_back(d_first_out, normed_one, scale_one, ln1_gain)
    d_first_low = d_first.astype(jnp.bfloat16)
    d_b_out = jnp.sum(d_first, axis=0)
    d_w_out = jnp.einsum("tc,td->cd", context_low, d_first_low, preferred_element_type=jnp.float32)
    d_context_low = jnp.einsum(
        "td,cd->tc", d_first_low, w_out, preferred_element_type=jnp.float32
    ).astype(jnp.bfloat16)
    d_context = d_context_low.astype(jnp.float32)
    d_context_heads = d_context.reshape(local_rows, heads_here, head_size)
    d_attn = attn_scale * (
        d_context_heads - attn_unit * jnp.sum(attn_unit * d_context_heads, axis=-1, keepdims=True)
    )
    d_attn_low = d_attn.astype(jnp.bfloat16)
    tap_terms = []
    for shift_at in range(kernel):
        summed = jnp.sum(
            d_context * same_list[shift_at] * value_rim[shift_at : shift_at + local_rows], axis=0
        )
        tap_terms.append(jnp.sum(summed.reshape(heads_here, head_size), axis=1))
    d_taps = jnp.stack(tap_terms, axis=1)
    context_rim = padded(d_context_low, (("seq", 0),), radius).astype(jnp.float32)
    d_value_conv = jnp.zeros((local_rows, columns), jnp.float32)
    for shift_at in range(kernel):
        lower = 2 * radius - shift_at
        same_rows = (rim_items[lower : lower + local_rows] == query_items).astype(jnp.float32)[
            :, None
        ]
        d_value_conv = (
            d_value_conv
            + tap_columns[shift_at] * same_rows * context_rim[lower : lower + local_rows]
        )
    value_heads = value_low.reshape(local_rows, heads_here, head_size)
    both_packed = jnp.concatenate(
        [packed, query_low.reshape(local_rows, columns), d_attn_low.reshape(local_rows, columns)],
        axis=1,
    )

    def pair_block(state, pieces, offset):
        d_query, d_keys, d_values = state
        block = pieces[0]
        count = block.shape[0]
        keys_block, values_block = split_pair(block[:, : 2 * columns])
        queries_block, d_attn_block = split_pair(block[:, 2 * columns :])
        other_items = item_index(offset + jnp.arange(count, dtype=jnp.int32), ends)
        same = (query_items[:, None] == other_items[None, :]).astype(jnp.float32)
        weights, d_scores = collision_back(query_low, keys_block, values_block, d_attn_low, same)
        d_query = d_query + jnp.einsum(
            "hbk,khe->bhe", d_scores, keys_block, preferred_element_type=jnp.float32
        )
        weights_own, d_scores_own = collision_back(
            queries_block, key_low, value_heads, d_attn_block, same.T
        )
        d_keys = d_keys + jnp.einsum(
            "hbk,bhe->khe", d_scores_own, queries_block, preferred_element_type=jnp.float32
        )
        d_values = d_values + jnp.einsum(
            "hbk,bhe->khe", weights_own, d_attn_block, preferred_element_type=jnp.float32
        )
        return (d_query, d_keys, d_values)

    zero_state = (zero_heads, zero_heads, zero_heads)
    d_query, d_key_unit, d_value_heads = fold_blocks(
        zero_state,
        (lax.all_gather(both_packed, "seq", axis=0, tiled=True),),
        jnp.int32(0),
        pair_block,
    )
    d_value_attn = d_value_heads.reshape(local_rows, columns)
    d_query_raw = query_scale * (
        d_query - query_unit * jnp.sum(query_unit * d_query, axis=-1, keepdims=True)
    )
    d_key_raw = key_scale * (
        d_key_unit - key_unit * jnp.sum(key_unit * d_key_unit, axis=-1, keepdims=True)
    )
    d_value = d_value_attn + d_value_conv
    d_projected_low = jnp.stack(
        [d_query_raw.reshape(local_rows, columns), d_key_raw.reshape(local_rows, columns), d_value]
    ).astype(jnp.bfloat16)
    d_bias_all = jnp.sum(d_projected_low.astype(jnp.float32), axis=1)
    d_b_qv = jnp.stack([d_bias_all[0], d_bias_all[2]])
    d_w_qkv = jnp.einsum("td,ite->ide", tokens, d_projected_low, preferred_element_type=jnp.float32)
    d_tokens_part = jnp.einsum(
        "ite,ide->td", d_projected_low, w_qkv, preferred_element_type=jnp.float32
    )
    d_tokens = (
        d_first + lax.psum(d_tokens_part.astype(jnp.bfloat16), "mp").astype(jnp.float32)
    ).astype(jnp.bfloat16)
    summed_grads = (
        lax.psum(d_w_qkv.astype(jnp.bfloat16), "seq").astype(jnp.float32),
        lax.psum(d_b_qv.astype(jnp.bfloat16), "seq").astype(jnp.float32),
        lax.psum(d_taps.astype(jnp.bfloat16), "seq").astype(jnp.float32),
        lax.psum(d_w_out.astype(jnp.bfloat16), "seq").astype(jnp.float32),
        lax.psum(d_b_out.astype(jnp.bfloat16), "seq").astype(jnp.float32),
        lax.psum(d_ln1_gain.astype(jnp.bfloat16), "seq").astype(jnp.float32),
        lax.psum(d_ln1_bias.astype(jnp.bfloat16), "seq").astype(jnp.float32),
        lax.psum(d_w_up.astype(jnp.bfloat16), "seq").astype(jnp.float32),
        lax.psum(d_b_up.astype(jnp.bfloat16), "seq").astype(jnp.float32),
        lax.psum(d_w_down.astype(jnp.bfloat16), "seq").astype(jnp.float32),
        lax.psum(d_b_down.astype(jnp.bfloat16), "seq").astype(jnp.float32),
        lax.psum(d_ln2_gain.astype(jnp.bfloat16), "seq").astype(jnp.float32),
        lax.psum(d_ln2_bias.astype(jnp.bfloat16), "seq").astype(jnp.float32),
    )
    return (layer_output, d_tokens) + tuple(summed_grads)


def solution(mesh):
    placed = (
        P("seq", None),
        P(),
        P(None, None, "mp"),
        P(None, "mp"),
        P("mp", None),
        P("mp", None),
        P(),
        P(),
        P(),
        P(None, "mp"),
        P("mp"),
        P("mp", None),
        P(),
        P(),
        P(),
        P("seq", None),
    )
    return jax.shard_map(
        per_device,
        mesh=mesh,
        in_specs=placed,
        out_specs=(
            P("seq", None),
            P("seq", None),
            P(None, None, "mp"),
            P(None, "mp"),
            P("mp", None),
            P("mp", None),
            P(),
            P(),
            P(),
            P(None, "mp"),
            P("mp"),
            P("mp", None),
            P(),
            P(),
            P(),
        ),
        check_vma=False,
    )
```

profile of v0, /device:TPU:0, one launch (start us, length us, event | category | flops | bytes accessed | tf_op | source)
XLA Modules:
  0.0 956.8 jit_solution(4926142767283352020)
XLA Ops:
  8.2 2.0 fusion.101
  14.3 4.9 collective-permute-start
  26.7 52.4 %all-gather.3.cloned.1.call-done = bf16[4096,384]{0,1:T(8,128)(2,1)} async-done(((bf16[512,384]{0,1:T(8,128)(2,1)}), bf16[4096,384]{0,1:T(8,128)(2,1)}) %all-gather.3.cloned.1.call-update) | async-done | bytes 3145744 | tf_op jit(solution)/shard_map/all_gather | solution.py:152
  79.1 4.0 copy.145
  83.5 89.9 %while.26 = (s32[]{:T(128)}, f32[512,3,64]{0,2,1:T(8,128)S(1)}, bf16[4,1024,384]{1,2,0:T(8,128)(2,1)}, s32[512]{0:T(512)S(1)}, s32[4]{0:T(128)S(1)}, /*index=5*/...) while((s32[]{:T(128)}, f32[512,3,64]{0,2,1:T(8,128)S(1)}, ...), condition=%wide.region_6.7_spmd.clone, body=%wide.region_4.6_spmd.clone.sunk | while | flops 421229568 | bytes 9136299 | solution.py:67
  86.9 1.5 compare_convert_fusion.4
  89.7 16.3 %fusion.364 = f32[512,3,64]{0,2,1:T(8,128)S(1)} fusion(bf16[1024,3,64]{0,2,1:T(8,128)(2,1)S(1)} %bitcast.400, f32[512,1024]{0,1:T(8,128)} %compare_convert_fusion.4, bf16[1024,3,64]{0,2,1:T(8,128)(2,1)S(1)} %bitcast.399, bf16[512,3,64]{0,2,1:T(8,128)(2,1)S(1)} %get-tuple-element.668, f32[512,3,64]{0,2,1:T(8,128)S(1)} %get-tuple-element.654, ...), kind=kOutput, calls=%fused_computation.16.clone.1 | convolution fusion | flops 420151296 | bytes 3866625 | tf_op jit(solution)/shard_map/while/body/eval_jaxpr/hbk,khe->bhe/dot_general | solution.py:147
  109.2 1.5 compare_convert_fusion.4
  112.0 16.3 %fusion.364 = f32[512,3,64]{0,2,1:T(8,128)S(1)} fusion(bf16[1024,3,64]{0,2,1:T(8,128)(2,1)S(1)} %bitcast.400, f32[512,1024]{0,1:T(8,128)} %compare_convert_fusion.4, bf16[1024,3,64]{0,2,1:T(8,128)(2,1)S(1)} %bitcast.399, bf16[512,3,64]{0,2,1:T(8,128)(2,1)S(1)} %get-tuple-element.668, f32[512,3,64]{0,2,1:T(8,128)S(1)} %get-tuple-element.654, ...), kind=kOutput, calls=%fused_computation.16.clone.1 | convolution fusion | flops 420151296 | bytes 3866625 | tf_op jit(solution)/shard_map/while/body/eval_jaxpr/hbk,khe->bhe/dot_general | solution.py:147
  134.3 16.3 %fusion.364 = f32[512,3,64]{0,2,1:T(8,128)S(1)} fusion(bf16[1024,3,64]{0,2,1:T(8,128)(2,1)S(1)} %bitcast.400, f32[512,1024]{0,1:T(8,128)} %compare_convert_fusion.4, bf16[1024,3,64]{0,2,1:T(8,128)(2,1)S(1)} %bitcast.399, bf16[512,3,64]{0,2,1:T(8,128)(2,1)S(1)} %get-tuple-element.668, f32[512,3,64]{0,2,1:T(8,128)S(1)} %get-tuple-element.654, ...), kind=kOutput, calls=%fused_computation.16.clone.1 | convolution fusion | flops 420151296 | bytes 3866625 | tf_op jit(solution)/shard_map/while/body/eval_jaxpr/hbk,khe->bhe/dot_general | solution.py:147
  156.7 16.3 %fusion.364 = f32[512,3,64]{0,2,1:T(8,128)S(1)} fusion(bf16[1024,3,64]{0,2,1:T(8,128)(2,1)S(1)} %bitcast.400, f32[512,1024]{0,1:T(8,128)} %compare_convert_fusion.4, bf16[1024,3,64]{0,2,1:T(8,128)(2,1)S(1)} %bitcast.399, bf16[512,3,64]{0,2,1:T(8,128)(2,1)S(1)} %get-tuple-element.668, f32[512,3,64]{0,2,1:T(8,128)S(1)} %get-tuple-element.654, ...), kind=kOutput, calls=%fused_computation.16.clone.1 | convolution fusion | flops 420151296 | bytes 3866625 | tf_op jit(solution)/shard_map/while/body/eval_jaxpr/hbk,khe->bhe/dot_general | solution.py:147
  174.7 5.9 fusion.241
  181.3 1.6 fusion.303
  183.0 41.1 %all-reduce.8.cloned.1.call-done = f32[512,768]{1,0:T(8,128)} async-done(((f32[512,768]{1,0:T(8,128)}), f32[512,768]{1,0:T(8,128)}) %all-reduce.8.cloned.1.call-update) | async-done | bytes 1572880 | tf_op jit(solution)/shard_map/psum | solution.py:169
  224.1 1.9 fusion.290
  226.7 5.1 fusion.87
  232.7 1.9 fusion.304
  234.7 43.0 %all-reduce.10.cloned.1.call-done = f32[512,768]{1,0:T(8,128)} async-done(((f32[512,768]{1,0:T(8,128)}), f32[512,768]{1,0:T(8,128)}) %all-reduce.10.cloned.1.call-update) | async-done | bytes 1572880 | tf_op jit(solution)/shard_map/psum | solution.py:175
  277.7 2.0 fusion.289
  282.2 2.1 fusion.286
  284.3 1.7 fusion.299
  286.9 2.0 fusion.305
  289.0 43.0 %all-reduce.12.cloned.1.call-done = f32[512,768]{1,0:T(8,128)} async-done(((f32[512,768]{1,0:T(8,128)}), f32[512,768]{1,0:T(8,128)}) %all-reduce.12.cloned.1.call-update) | async-done | bytes 1572880 | tf_op jit(solution)/shard_map/psum | solution.py:192
  332.0 3.3 multiply_reduce_fusion
  336.4 1.9 fusion.219
  340.3 3.3 convolution_convert_fusion.1
  343.6 3.4 collective-permute-start.2
  348.3 1.8 convolution_convert_fusion
  350.2 3.8 collective-permute-done.3
  354.9 85.7 %all-gather.5.cloned.1.call-done = bf16[4096,768]{0,1:T(8,128)(2,1)} async-done(((bf16[512,768]{0,1:T(8,128)(2,1)}), bf16[4096,768]{0,1:T(8,128)(2,1)}) %all-gather.5.cloned.1.call-update) | async-done | bytes 6291472 | tf_op jit(solution)/shard_map/all_gather | solution.py:256
  440.7 6.4 copy.144
  447.1 304.2 %while.27 = (s32[]{:T(128)}, f32[512,3,64]{0,2,1:T(8,128)}, f32[512,3,64]{0,2,1:T(8,128)}, f32[512,3,64]{0,2,1:T(8,128)}, bf16[4,1024,768]{1,2,0:T(8,128)(2,1)},...) while((s32[]{:T(128)}, f32[512,3,64]{0,2,1:T(8,128)}, ...), condition=%wide.region_23.24_spmd.clone, body=%wide.region_21.23_spmd.clone.sunk | while | flops 1486976000 | bytes 64526712 | solution.py:67
  450.8 1.5 dynamic-slice_bitcast_fusion.5
  453.3 3.7 fusion.381
  457.0 21.5 %fusion.382 = f32[512,3,64]{0,2,1:T(8,128)} fusion(bf16[1024,3,64]{0,2,1:T(8,128)(2,1)S(1)} %bitcast.393, f32[3,1024,512]{2,1,0:T(8,128)} %fusion.381, f32[1024,512]{1,0:T(8,128)S(1)} %compare_select_fusion.5, bf16[1024,3,64]{0,2,1:T(8,128)(2,1)} %bitcast.397, bf16[512,3,64]{0,2,1:T(8,128)(2,1)} %get-tuple-element.709, ...), kind=kOutput, calls=%fused_computation.66.clone.1 | convolution fusion | flops 431161344 | bytes 10158081 | tf_op jit(solution)/shard_map/while/body/eval_jaxpr/hbk,bhe->khe/dot_general | solution.py:245
  479.6 15.2 %fusion.383 = f32[512,3,64]{0,2,1:T(8,128)S(1)} fusion(bf16[1024,3,64]{0,2,1:T(8,128)(2,1)S(1)} %bitcast.398, f32[3,1024,512]{2,1,0:T(8,128)} %fusion.381, f32[1024,512]{1,0:T(8,128)S(1)} %compare_convert_fusion.5, f32[512,3,64]{0,2,1:T(8,128)S(1)} %copy-done.37, pred[]{:T(512)S(6)} %compare.7), kind=kOutput, calls=%fused_computation.65.clone.1 | convolution fusion | flops 218824704 | bytes 9568257 | tf_op jit(solution)/shard_map/while/body/eval_jaxpr/hbk,bhe->khe/dot_general | solution.py:248
  495.0 3.7 fusion.379
  498.7 21.1 %fusion.380 = f32[512,3,64]{0,2,1:T(8,128)S(1)} fusion(bf16[1024,3,64]{0,2,1:T(8,128)(2,1)S(1)} %bitcast.396, f32[3,1024,512]{2,1,0:T(8,128)} %fusion.379, f32[512,1024]{0,1:T(8,128)S(1)} %compare_select_fusion.4, bf16[512,3,64]{0,2,1:T(8,128)(2,1)} %get-tuple-element.708, f32[512,3,64]{0,2,1:T(8,128)S(1)} %copy-done.40, pred[]{:T(512)S(6)} %compare.7), kind=kOutput, calls=%fused_computation.67.clone.1 | convolution fusion | flops 431161344 | bytes 9764865 | tf_op jit(solution)/shard_map/while/body/eval_jaxpr/hbk,khe->bhe/dot_general | solution.py:239
  524.9 1.5 dynamic-slice_bitcast_fusion.5
  527.4 3.7 fusion.381
  531.1 21.3 %fusion.382 = f32[512,3,64]{0,2,1:T(8,128)} fusion(bf16[1024,3,64]{0,2,1:T(8,128)(2,1)S(1)} %bitcast.393, f32[3,1024,512]{2,1,0:T(8,128)} %fusion.381, f32[1024,512]{1,0:T(8,128)S(1)} %compare_select_fusion.5, bf16[1024,3,64]{0,2,1:T(8,128)(2,1)} %bitcast.397, bf16[512,3,64]{0,2,1:T(8,128)(2,1)} %get-tuple-element.709, ...), kind=kOutput, calls=%fused_computation.66.clone.1 | convolution fusion | flops 431161344 | bytes 10158081 | tf_op jit(solution)/shard_map/while/body/eval_jaxpr/hbk,bhe->khe/dot_general | solution.py:245
  553.5 15.2 %fusion.383 = f32[512,3,64]{0,2,1:T(8,128)S(1)} fusion(bf16[1024,3,64]{0,2,1:T(8,128)(2,1)S(1)} %bitcast.398, f32[3,1024,512]{2,1,0:T(8,128)} %fusion.381, f32[1024,512]{1,0:T(8,128)S(1)} %compare_convert_fusion.5, f32[512,3,64]{0,2,1:T(8,128)S(1)} %copy-done.37, pred[]{:T(512)S(6)} %compare.7), kind=kOutput, calls=%fused_computation.65.clone.1 | convolution fusion | flops 218824704 | bytes 9568257 | tf_op jit(solution)/shard_map/while/body/eval_jaxpr/hbk,bhe->khe/dot_general | solution.py:248
  568.9 3.7 fusion.379
  572.6 21.3 %fusion.380 = f32[512,3,64]{0,2,1:T(8,128)S(1)} fusion(bf16[1024,3,64]{0,2,1:T(8,128)(2,1)S(1)} %bitcast.396, f32[3,1024,512]{2,1,0:T(8,128)} %fusion.379, f32[512,1024]{0,1:T(8,128)S(1)} %compare_select_fusion.4, bf16[512,3,64]{0,2,1:T(8,128)(2,1)} %get-tuple-element.708, f32[512,3,64]{0,2,1:T(8,128)S(1)} %copy-done.40, pred[]{:T(512)S(6)} %compare.7), kind=kOutput, calls=%fused_computation.67.clone.1 | convolution fusion | flops 431161344 | bytes 9764865 | tf_op jit(solution)/shard_map/while/body/eval_jaxpr/hbk,khe->bhe/dot_general | solution.py:239
  598.8 1.5 dynamic-slice_bitcast_fusion.5
  601.3 3.7 fusion.381
  604.9 21.5 %fusion.382 = f32[512,3,64]{0,2,1:T(8,128)} fusion(bf16[1024,3,64]{0,2,1:T(8,128)(2,1)S(1)} %bitcast.393, f32[3,1024,512]{2,1,0:T(8,128)} %fusion.381, f32[1024,512]{1,0:T(8,128)S(1)} %compare_select_fusion.5, bf16[1024,3,64]{0,2,1:T(8,128)(2,1)} %bitcast.397, bf16[512,3,64]{0,2,1:T(8,128)(2,1)} %get-tuple-element.709, ...), kind=kOutput, calls=%fused_computation.66.clone.1 | convolution fusion | flops 431161344 | bytes 10158081 | tf_op jit(solution)/shard_map/while/body/eval_jaxpr/hbk,bhe->khe/dot_general | solution.py:245
  627.6 15.2 %fusion.383 = f32[512,3,64]{0,2,1:T(8,128)S(1)} fusion(bf16[1024,3,64]{0,2,1:T(8,128)(2,1)S(1)} %bitcast.398, f32[3,1024,512]{2,1,0:T(8,128)} %fusion.381, f32[1024,512]{1,0:T(8,128)S(1)} %compare_convert_fusion.5, f32[512,3,64]{0,2,1:T(8,128)S(1)} %copy-done.37, pred[]{:T(512)S(6)} %compare.7), kind=kOutput, calls=%fused_computation.65.clone.1 | convolution fusion | flops 218824704 | bytes 9568257 | tf_op jit(solution)/shard_map/while/body/eval_jaxpr/hbk,bhe->khe/dot_general | solution.py:248
  643.0 3.7 fusion.379
  646.7 21.1 %fusion.380 = f32[512,3,64]{0,2,1:T(8,128)S(1)} fusion(bf16[1024,3,64]{0,2,1:T(8,128)(2,1)S(1)} %bitcast.396, f32[3,1024,512]{2,1,0:T(8,128)} %fusion.379, f32[512,1024]{0,1:T(8,128)S(1)} %compare_select_fusion.4, bf16[512,3,64]{0,2,1:T(8,128)(2,1)} %get-tuple-element.708, f32[512,3,64]{0,2,1:T(8,128)S(1)} %copy-done.40, pred[]{:T(512)S(6)} %compare.7), kind=kOutput, calls=%fused_computation.67.clone.1 | convolution fusion | flops 431161344 | bytes 9764865 | tf_op jit(solution)/shard_map/while/body/eval_jaxpr/hbk,khe->bhe/dot_general | solution.py:239
  672.9 1.5 dynamic-slice_bitcast_fusion.5
  675.4 3.7 fusion.381
  679.1 21.3 %fusion.382 = f32[512,3,64]{0,2,1:T(8,128)} fusion(bf16[1024,3,64]{0,2,1:T(8,128)(2,1)S(1)} %bitcast.393, f32[3,1024,512]{2,1,0:T(8,128)} %fusion.381, f32[1024,512]{1,0:T(8,128)S(1)} %compare_select_fusion.5, bf16[1024,3,64]{0,2,1:T(8,128)(2,1)} %bitcast.397, bf16[512,3,64]{0,2,1:T(8,128)(2,1)} %get-tuple-element.709, ...), kind=kOutput, calls=%fused_computation.66.clone.1 | convolution fusion | flops 431161344 | bytes 10158081 | tf_op jit(solution)/shard_map/while/body/eval_jaxpr/hbk,bhe->khe/dot_general | solution.py:245
  701.5 15.2 %fusion.383 = f32[512,3,64]{0,2,1:T(8,128)S(1)} fusion(bf16[1024,3,64]{0,2,1:T(8,128)(2,1)S(1)} %bitcast.398, f32[3,1024,512]{2,1,0:T(8,128)} %fusion.381, f32[1024,512]{1,0:T(8,128)S(1)} %compare_convert_fusion.5, f32[512,3,64]{0,2,1:T(8,128)S(1)} %copy-done.37, pred[]{:T(512)S(6)} %compare.7), kind=kOutput, calls=%fused_computation.65.clone.1 | convolution fusion | flops 218824704 | bytes 9568257 | tf_op jit(solution)/shard_map/while/body/eval_jaxpr/hbk,bhe->khe/dot_general | solution.py:248
  716.9 3.7 fusion.379
  720.6 21.3 %fusion.380 = f32[512,3,64]{0,2,1:T(8,128)S(1)} fusion(bf16[1024,3,64]{0,2,1:T(8,128)(2,1)S(1)} %bitcast.396, f32[3,1024,512]{2,1,0:T(8,128)} %fusion.379, f32[512,1024]{0,1:T(8,128)S(1)} %compare_select_fusion.4, bf16[512,3,64]{0,2,1:T(8,128)(2,1)} %get-tuple-element.708, f32[512,3,64]{0,2,1:T(8,128)S(1)} %copy-done.40, pred[]{:T(512)S(6)} %compare.7), kind=kOutput, calls=%fused_computation.67.clone.1 | convolution fusion | flops 431161344 | bytes 9764865 | tf_op jit(solution)/shard_map/while/body/eval_jaxpr/hbk,khe->bhe/dot_general | solution.py:239
  755.1 6.0 fusion.242
  761.2 3.0 bitcast_convert_fusion
  765.3 1.5 fusion.103
  783.4 34.6 %all-reduce = (bf16[2,192]{1,0:T(2,128)(2,1)S(1)}, bf16[3,33]{1,0:T(4,128)(2,1)S(1)}, bf16[768]{0:T(1024)(128)(2,1)S(1)}, bf16[768]{0:T(1024)(128)(2,1)S(1)}, bf...) all-reduce(bf16[2,192]{1,0:T(2,128)(2,1)S(1)} %pad_maximum_fusion.4, ...), channel_id=1, replica_groups=mesh['seq'=8,'mp'=4] {'seq'}, use_global_device_ids=true, to_apply=%region_29.30 | all-reduce | flops 5859 | bytes 23436 | tf_op jit(solution)/shard_map/psum | solution.py:282
  823.3 2.2 add_convert_fusion
  825.5 117.4 %all-reduce.16.cloned.1.call-done = (bf16[3,768,192]{1,2,0:T(8,128)(2,1)}, bf16[192,768]{1,0:T(8,128)(2,1)}, bf16[768,768]{1,0:T(8,128)(2,1)}, bf16[768,768]{1,0:T(8,128)(2,1)}) async-done(((bf16[3,768,192]{1,2,0:T(8,128)(2,1)}, bf16[192,768]{1,0:T(8,128)(2,1)}, bf16[768,768]{1,0:T(8,128)(2,1)}, bf16[768,768]{1,0:T(8,128)(2,1)}), (bf16[3,768,192]{1,2,0:T(8,128)(2,1)}, bf16[192,768]{1,0:T(8,128)(2,1)}, ...) | async-done | bytes 3538960 | tf_op jit(solution)/shard_map/psum | solution.py:281
  942.9 2.9 convert_element_type.398
  945.9 1.6 convert_element_type.401
  (689 shorter events, 98.8 us)
Async XLA Ops:
  7.2 219.2 %copy-start = (bf16[768,768]{1,0:T(8,128)(2,1)S(1)}, bf16[768,768]{1,0:T(8,128)(2,1)}, u32[]{:S(2)}) copy-start(bf16[768,768]{1,0:T(8,128)(2,1)} %param.29) | copy-start | bytes 3538948
  7.2 71.9 %all-gather.3.cloned.1.call-start = ((), (), s32[]{:S(2)}) async-start(), calls=%async_computation | async-start | bytes 3538944 | tf_op jit(solution)/shard_map/all_gather | solution.py:152
  11.2 328.3 %copy-start.46 = (f32[512,3]{0,1:T(4,128)}, f32[512,3]{0,1:T(4,128)S(1)}, u32[]{:S(2)}) copy-start(f32[512,3]{0,1:T(4,128)S(1)} %get-tuple-element.515) | copy-start | bytes 18436
  13.4 210.7 %all-reduce.8.cloned.1.call-start = ((), (), s32[]{:S(2)}) async-start(), calls=%async_computation.1 | async-start | bytes 3145728 | tf_op jit(solution)/shard_map/psum | solution.py:169
  14.3 12.2 %collective-permute-start = (bf16[16,192]{0,1:T(8,128)(2,1)S(1)}, bf16[16,192]{0,1:T(8,128)(2,1)S(1)}, u32[]{:S(2)}, u32[]{:S(2)}) collective-permute-start(bf16[16,192]{0,1:T(8,128)(2,1)S(1)} %get-tuple-element.438), channel_id=1, source_target_pairs={{0,4},{4,8},{8,12},{12,16},{16,20},{20,24},{24,28},{1,5},{5,9},{9,... | collective-permute-start | bytes 18440 | tf_op jit(solution)/shard_map/ppermute | solution.py:20
  19.2 7.4 collective-permute-start.1
  25.6 148.5 %copy-start.77 = (f32[512]{0:T(512)}, f32[512]{0:T(512)S(1)}, u32[]{:S(2)}) copy-start(f32[512]{0:T(512)S(1)} %get-tuple-element.492) | copy-start | bytes 6148
  25.6 148.5 %copy-start.80 = (f32[512]{0:T(512)}, f32[512]{0:T(512)S(1)}, u32[]{:S(2)}) copy-start(f32[512]{0:T(512)S(1)} %get-tuple-element.493) | copy-start | bytes 6148
  25.6 148.6 %copy-start.83 = (f32[512]{0:T(512)}, f32[512]{0:T(512)S(1)}, u32[]{:S(2)}) copy-start(f32[512]{0:T(512)S(1)} %get-tuple-element.494) | copy-start | bytes 6148
  25.6 148.6 %copy-start.86 = (f32[512]{0:T(512)}, f32[512]{0:T(512)S(1)}, u32[]{:S(2)}) copy-start(f32[512]{0:T(512)S(1)} %get-tuple-element.495) | copy-start | bytes 6148
  25.6 148.6 %copy-start.89 = (f32[512]{0:T(512)}, f32[512]{0:T(512)S(1)}, u32[]{:S(2)}) copy-start(f32[512]{0:T(512)S(1)} %get-tuple-element.496) | copy-start | bytes 6148
  25.6 148.6 %copy-start.92 = (f32[512]{0:T(512)}, f32[512]{0:T(512)S(1)}, u32[]{:S(2)}) copy-start(f32[512]{0:T(512)S(1)} %get-tuple-element.497) | copy-start | bytes 6148
  25.6 148.6 %copy-start.95 = (f32[512]{0:T(512)}, f32[512]{0:T(512)S(1)}, u32[]{:S(2)}) copy-start(f32[512]{0:T(512)S(1)} %get-tuple-element.498) | copy-start | bytes 6148
  25.6 148.6 %copy-start.98 = (f32[512]{0:T(512)}, f32[512]{0:T(512)S(1)}, u32[]{:S(2)}) copy-start(f32[512]{0:T(512)S(1)} %get-tuple-element.499) | copy-start | bytes 6148
  26.3 147.9 %copy-start.51 = (f32[512]{0:T(512)}, f32[512]{0:T(512)S(1)}, u32[]{:S(2)}) copy-start(f32[512]{0:T(512)S(1)} %get-tuple-element.475) | copy-start | bytes 6148
  26.3 147.9 %copy-start.53 = (f32[512]{0:T(512)}, f32[512]{0:T(512)S(1)}, u32[]{:S(2)}) copy-start(f32[512]{0:T(512)S(1)} %get-tuple-element.476) | copy-start | bytes 6148
  26.4 147.9 %copy-start.55 = (f32[512]{0:T(512)}, f32[512]{0:T(512)S(1)}, u32[]{:S(2)}) copy-start(f32[512]{0:T(512)S(1)} %get-tuple-element.483) | copy-start | bytes 6148
  26.4 147.9 %copy-start.57 = (f32[512]{0:T(512)}, f32[512]{0:T(512)S(1)}, u32[]{:S(2)}) copy-start(f32[512]{0:T(512)S(1)} %get-tuple-element.484) | copy-start | bytes 6148
  26.4 147.9 %copy-start.59 = (f32[512]{0:T(512)}, f32[512]{0:T(512)S(1)}, u32[]{:S(2)}) copy-start(f32[512]{0:T(512)S(1)} %get-tuple-element.485) | copy-start | bytes 6148
  26.4 147.9 %copy-start.62 = (f32[512]{0:T(512)}, f32[512]{0:T(512)S(1)}, u32[]{:S(2)}) copy-start(f32[512]{0:T(512)S(1)} %get-tuple-element.486) | copy-start | bytes 6148
  26.4 147.9 %copy-start.65 = (f32[512]{0:T(512)}, f32[512]{0:T(512)S(1)}, u32[]{:S(2)}) copy-start(f32[512]{0:T(512)S(1)} %get-tuple-element.487) | copy-start | bytes 6148
  26.4 147.9 %copy-start.68 = (f32[512]{0:T(512)}, f32[512]{0:T(512)S(1)}, u32[]{:S(2)}) copy-start(f32[512]{0:T(512)S(1)} %get-tuple-element.488) | copy-start | bytes 6148
  26.4 147.9 %copy-start.71 = (f32[512]{0:T(512)}, f32[512]{0:T(512)S(1)}, u32[]{:S(2)}) copy-start(f32[512]{0:T(512)S(1)} %get-tuple-element.489) | copy-start | bytes 6148
  26.4 147.9 %copy-start.74 = (f32[512]{0:T(512)}, f32[512]{0:T(512)S(1)}, u32[]{:S(2)}) copy-start(f32[512]{0:T(512)S(1)} %get-tuple-element.490) | copy-start | bytes 6148
  26.4 147.9 %copy-start.101 = (f32[512]{0:T(512)}, f32[512]{0:T(512)S(1)}, u32[]{:S(2)}) copy-start(f32[512]{0:T(512)S(1)} %get-tuple-element.477) | copy-start | bytes 6148
  26.4 147.9 %copy-start.104 = (f32[512]{0:T(512)}, f32[512]{0:T(512)S(1)}, u32[]{:S(2)}) copy-start(f32[512]{0:T(512)S(1)} %get-tuple-element.478) | copy-start | bytes 6148
  26.5 147.9 %copy-start.107 = (f32[512]{0:T(512)}, f32[512]{0:T(512)S(1)}, u32[]{:S(2)}) copy-start(f32[512]{0:T(512)S(1)} %get-tuple-element.479) | copy-start | bytes 6148
  26.5 147.9 %copy-start.110 = (f32[512]{0:T(512)}, f32[512]{0:T(512)S(1)}, u32[]{:S(2)}) copy-start(f32[512]{0:T(512)S(1)} %get-tuple-element.480) | copy-start | bytes 6148
  26.7 309.6 %copy-start.2 = (f32[544,192]{0,1:T(8,128)}, f32[544,192]{0,1:T(8,128)S(1)}, u32[]{:S(2)}) copy-start(f32[544,192]{0,1:T(8,128)S(1)} %maximum_convert_fusion) | copy-start | bytes 1253380
  83.1 91.3 %copy-start.121 = (f32[512]{0:T(512)S(1)}, f32[512]{0:T(512)}, u32[]{:S(2)}) copy-start(f32[512]{0:T(512)} %get-tuple-element.474) | copy-start | bytes 6148
  83.1 91.3 %copy-start.123 = (f32[512]{0:T(512)S(1)}, f32[512]{0:T(512)}, u32[]{:S(2)}) copy-start(f32[512]{0:T(512)} %get-tuple-element.423) | copy-start | bytes 6148
  83.1 91.3 %copy-start.125 = (f32[512]{0:T(512)S(1)}, f32[512]{0:T(512)}, u32[]{:S(2)}) copy-start(f32[512]{0:T(512)} %get-tuple-element.491) | copy-start | bytes 6148
  83.2 91.3 %copy-start.127 = (f32[512]{0:T(512)S(1)}, f32[512]{0:T(512)}, u32[]{:S(2)}) copy-start(f32[512]{0:T(512)} %get-tuple-element.500) | copy-start | bytes 6148
  83.2 91.3 %copy-start.129 = (f32[512]{0:T(512)S(1)}, f32[512]{0:T(512)}, u32[]{:S(2)}) copy-start(f32[512]{0:T(512)} %get-tuple-element.501) | copy-start | bytes 6148
  83.2 91.3 %copy-start.131 = (f32[512]{0:T(512)S(1)}, f32[512]{0:T(512)}, u32[]{:S(2)}) copy-start(f32[512]{0:T(512)} %get-tuple-element.502) | copy-start | bytes 6148
  83.2 91.3 %copy-start.133 = (f32[512]{0:T(512)S(1)}, f32[512]{0:T(512)}, u32[]{:S(2)}) copy-start(f32[512]{0:T(512)} %get-tuple-element.503) | copy-start | bytes 6148
  83.2 91.3 %copy-start.135 = (f32[512]{0:T(512)S(1)}, f32[512]{0:T(512)}, u32[]{:S(2)}) copy-start(f32[512]{0:T(512)} %get-tuple-element.504) | copy-start | bytes 6148
  83.2 91.3 %copy-start.138 = (f32[1,192]{1,0:T(1,128)S(1)}, f32[1,192]{1,0:T(1,128)}, u32[]{:S(2)}) copy-start(f32[1,192]{1,0:T(1,128)} %get-tuple-element.459) | copy-start | bytes 2308
  83.2 91.3 %copy-start.140 = (f32[1,192]{1,0:T(1,128)S(1)}, f32[1,192]{1,0:T(1,128)}, u32[]{:S(2)}) copy-start(f32[1,192]{1,0:T(1,128)} %get-tuple-element.460) | copy-start | bytes 2308
  83.2 91.3 %copy-start.142 = (f32[1,192]{1,0:T(1,128)S(1)}, f32[1,192]{1,0:T(1,128)}, u32[]{:S(2)}) copy-start(f32[1,192]{1,0:T(1,128)} %get-tuple-element.461) | copy-start | bytes 2308
  83.2 91.3 %copy-start.144 = (f32[1,192]{1,0:T(1,128)S(1)}, f32[1,192]{1,0:T(1,128)}, u32[]{:S(2)}) copy-start(f32[1,192]{1,0:T(1,128)} %get-tuple-element.462) | copy-start | bytes 2308
  83.2 91.3 %copy-start.145 = (f32[1,192]{1,0:T(1,128)S(1)}, f32[1,192]{1,0:T(1,128)}, u32[]{:S(2)}) copy-start(f32[1,192]{1,0:T(1,128)} %get-tuple-element.463) | copy-start | bytes 2308
  83.3 91.3 %copy-start.146 = (f32[1,192]{1,0:T(1,128)S(1)}, f32[1,192]{1,0:T(1,128)}, u32[]{:S(2)}) copy-start(f32[1,192]{1,0:T(1,128)} %get-tuple-element.464) | copy-start | bytes 2308
  83.3 91.3 %copy-start.147 = (f32[1,192]{1,0:T(1,128)S(1)}, f32[1,192]{1,0:T(1,128)}, u32[]{:S(2)}) copy-start(f32[1,192]{1,0:T(1,128)} %get-tuple-element.465) | copy-start | bytes 2308
  83.3 91.3 %copy-start.148 = (f32[1,192]{1,0:T(1,128)S(1)}, f32[1,192]{1,0:T(1,128)}, u32[]{:S(2)}) copy-start(f32[1,192]{1,0:T(1,128)} %get-tuple-element.466) | copy-start | bytes 2308
  83.3 91.3 %copy-start.149 = (f32[1,192]{1,0:T(1,128)S(1)}, f32[1,192]{1,0:T(1,128)}, u32[]{:S(2)}) copy-start(f32[1,192]{1,0:T(1,128)} %get-tuple-element.467) | copy-start | bytes 2308
  83.3 91.3 %copy-start.150 = (f32[1,192]{1,0:T(1,128)S(1)}, f32[1,192]{1,0:T(1,128)}, u32[]{:S(2)}) copy-start(f32[1,192]{1,0:T(1,128)} %get-tuple-element.468) | copy-start | bytes 2308
  83.3 91.3 %copy-start.151 = (f32[1,192]{1,0:T(1,128)S(1)}, f32[1,192]{1,0:T(1,128)}, u32[]{:S(2)}) copy-start(f32[1,192]{1,0:T(1,128)} %get-tuple-element.469) | copy-start | bytes 2308
  83.3 91.3 %copy-start.152 = (f32[1,192]{1,0:T(1,128)S(1)}, f32[1,192]{1,0:T(1,128)}, u32[]{:S(2)}) copy-start(f32[1,192]{1,0:T(1,128)} %get-tuple-element.470) | copy-start | bytes 2308
  83.3 91.3 %copy-start.153 = (f32[1,192]{1,0:T(1,128)S(1)}, f32[1,192]{1,0:T(1,128)}, u32[]{:S(2)}) copy-start(f32[1,192]{1,0:T(1,128)} %get-tuple-element.471) | copy-start | bytes 2308
  83.3 91.3 %copy-start.154 = (f32[1,192]{1,0:T(1,128)S(1)}, f32[1,192]{1,0:T(1,128)}, u32[]{:S(2)}) copy-start(f32[1,192]{1,0:T(1,128)} %get-tuple-element.472) | copy-start | bytes 2308
  83.3 91.3 %copy-start.155 = (f32[1,192]{1,0:T(1,128)S(1)}, f32[1,192]{1,0:T(1,128)}, u32[]{:S(2)}) copy-start(f32[1,192]{1,0:T(1,128)} %get-tuple-element.440) | copy-start | bytes 2308
  83.4 91.3 %copy-start.156 = (f32[1,192]{1,0:T(1,128)S(1)}, f32[1,192]{1,0:T(1,128)}, u32[]{:S(2)}) copy-start(f32[1,192]{1,0:T(1,128)} %get-tuple-element.441) | copy-start | bytes 2308
  83.4 91.3 %copy-start.157 = (f32[1,192]{1,0:T(1,128)S(1)}, f32[1,192]{1,0:T(1,128)}, u32[]{:S(2)}) copy-start(f32[1,192]{1,0:T(1,128)} %get-tuple-element.442) | copy-start | bytes 2308
  83.4 91.3 %copy-start.158 = (f32[1,192]{1,0:T(1,128)S(1)}, f32[1,192]{1,0:T(1,128)}, u32[]{:S(2)}) copy-start(f32[1,192]{1,0:T(1,128)} %get-tuple-element.443) | copy-start | bytes 2308
  182.9 94.8 %all-reduce.10.cloned.1.call-start = ((), (), s32[]{:S(2)}) async-start(), calls=%async_computation.2 | async-start | bytes 3145728 | tf_op jit(solution)/shard_map/psum | solution.py:175
  234.7 97.3 %all-reduce.12.cloned.1.call-start = ((), (), s32[]{:S(2)}) async-start(), calls=%async_computation.3 | async-start | bytes 3145728 | tf_op jit(solution)/shard_map/psum | solution.py:192
  288.9 151.7 %all-gather.5.cloned.1.call-start = ((), (), s32[]{:S(2)}) async-start(), calls=%async_computation.4 | async-start | bytes 7077888 | tf_op jit(solution)/shard_map/all_gather | solution.py:256
  339.4 483.9 %all-reduce.14.cloned.1.call-start = ((), (), s32[]{:S(2)}) async-start(), calls=%async_computation.5 | async-start | bytes 1572864 | tf_op jit(solution)/shard_map/psum | solution.py:278
  343.6 6.5 collective-permute-start.2
  347.0 7.0 collective-permute-start.3
  447.1 304.6 %copy-start.49 = (f32[512,3]{0,1:T(4,128)S(1)}, f32[512,3]{0,1:T(4,128)}, u32[]{:S(2)}) copy-start(f32[512,3]{0,1:T(4,128)} %copy-done.48) | copy-start | bytes 18436
  447.1 306.1 %copy-start.47 = (f32[512,3]{0,1:T(4,128)S(1)}, f32[512,3]{0,1:T(4,128)}, u32[]{:S(2)}) copy-start(f32[512,3]{0,1:T(4,128)} %copy-done.46) | copy-start | bytes 18436
  764.2 178.7 %all-reduce.16.cloned.1.call-start = ((), (), s32[]{:S(2)}) async-start(), calls=%async_computation.6 | async-start | bytes 7077888 | tf_op jit(solution)/shard_map/psum | solution.py:281
  (161 other events, 1739.2 us)
Sparse Core Ops, SparseCore 0:
  13.6 65.5 all-gather.2
  183.0 41.0 all-reduce.7
  234.8 42.8 all-reduce.9
  289.0 42.9 all-reduce.11
  339.6 101.0 all-gather.4
  764.3 32.8 all-reduce.13
  802.3 140.5 all-reduce.15
where the time goes:
time: 961 us; the launch traced here: 957 us
  waiting for transfers between devices  387 us (40%)
  matrix products  353 us (37%)
  other arithmetic  82.8 us (9%)
  local copies, waits for them, and re-layouts  59.3 us (6%)
  blocking collectives  34.6 us (4%)
  between operations  17.1 us (2%)
  loops' own time  12.2 us (1%)
  starting transfers between devices  11.1 us (1%)
    psum x1, waiting for transfers between devices, per_device(): lax.psum(d_w_qkv.astype(jnp.bfloat16), 'seq').astype(jnp.float32)  117 us
    all_gather x1, waiting for transfers between devices, per_device(): lax.all_gather(both_packed, 'seq', axis=0, tiled=True)  85.7 us
    dot_general x4, matrix products, pair_block(): jnp.einsum('hbk,bhe->khe', d_scores_own, queries_block, preferred_element...  85.6 us
    dot_general x4, matrix products, pair_block(): jnp.einsum('hbk,khe->bhe', d_scores, keys_block, preferred_element_type=j...  84.9 us
    dot_general x4, matrix products, attend(): jnp.einsum('hbk,khe->bhe', weights, values_heads, preferred_element_type=...  65.3 us
    dot_general x4, matrix products, pair_block(): jnp.einsum('hbk,bhe->khe', weights_own, d_attn_block, preferred_element_t...  60.7 us
    all_gather x1, waiting for transfers between devices, per_device(): lax.all_gather(packed, 'seq', axis=0, tiled=True)  52.4 us
    psum x1, waiting for transfers between devices, per_device(): d_first_out = d_second + lax.psum(d_first_part, 'mp')  43 us
  transfers between devices with their start and end apart: 11, of which 7 were waited for; matrix products, arithmetic and copies ran while one was open for 4% of the time, Pallas kernels for 0%

commit v1 on v0

--- a/solution.py
+++ b/solution.py
@@ -7,6 +7,18 @@
 SHRINK = 0.95
 NORM_EPS = 1e-06
 LAYER_EPS = 1e-05
+
+
+def collect(array, axis, dim):
+    ways, here = (lax.axis_size(axis), lax.axis_index(axis))
+    grown, reach = (array, 1)
+    while reach < ways:
+        theirs = lax.ppermute(grown, axis, [(d, d ^ reach) for d in range(ways)])
+        mine_first = jnp.concatenate([grown, theirs], axis=dim)
+        theirs_first = jnp.concatenate([theirs, grown], axis=dim)
+        grown = jnp.where(here & reach == 0, mine_first, theirs_first)
+        reach = 2 * reach
+    return grown
 
 
 def padded(cells, sides, width):
@@ -252,10 +264,7 @@
 
     zero_state = (zero_heads, zero_heads, zero_heads)
     d_query, d_key_unit, d_value_heads = fold_blocks(
-        zero_state,
-        (lax.all_gather(both_packed, "seq", axis=0, tiled=True),),
-        jnp.int32(0),
-        pair_block,
+        zero_state, (collect(both_packed, "seq", 0),), jnp.int32(0), pair_block
     )
     d_value_attn = d_value_heads.reshape(local_rows, columns)
     d_query_raw = query_scale * (

time: 961 us -> 1070 us (1.11)
  waiting for transfers between devices: 387 us -> 474 us
  other arithmetic: 82.8 us -> 105 us
    ppermute x0 -> x3, waiting for transfers between devices: none -> 172 us  [collect(): theirs = lax.ppermute(grown, axis, [(d, d ^ reach) for d in range(ways)])]
    all_gather x1 -> x0, waiting for transfers between devices: 85.7 us -> none  [per_device(): lax.all_gather(both_packed, 'seq', axis=0, tiled=True)]
    select_n x0 -> x3, other arithmetic: none -> 23.3 us  [collect(): grown = jnp.where(here & reach == 0, mine_first, theirs_first)]
  transfers between devices with their start and end apart: 11 -> 13, of which waited for: 7 -> 9; matrix products, arithmetic and copies ran while one was open for 4% -> 3% of each run, Pallas kernels for 0% -> 0%
where the time goes in v1:
time: 1070 us
  waiting for transfers between devices  474 us (44%)
  matrix products  353 us (33%)
  other arithmetic  105 us (10%)
  local copies, waits for them, and re-layouts  55.8 us (5%)
  blocking collectives  37.1 us (3%)
  starting transfers between devices  16.7 us (2%)
  between operations  16.5 us (2%)
  loops' own time  12.4 us (1%)
    ppermute x3, waiting for transfers between devices, collect(): theirs = lax.ppermute(grown, axis, [(d, d ^ reach) for d in range(ways)])  172 us
    psum x1, waiting for transfers between devices, per_device(): lax.psum(d_w_qkv.astype(jnp.bfloat16), 'seq').astype(jnp.float32)  118 us
    dot_general x4, matrix products, pair_block(): jnp.einsum('hbk,bhe->khe', d_scores_own, queries_block, preferred_element...  85.6 us
    dot_general x4, matrix products, pair_block(): jnp.einsum('hbk,khe->bhe', d_scores, keys_block, preferred_element_type=j...  84.9 us
    dot_general x4, matrix products, attend(): jnp.einsum('hbk,khe->bhe', weights, values_heads, preferred_element_type=...  65.3 us
    dot_general x4, matrix products, pair_block(): jnp.einsum('hbk,bhe->khe', weights_own, d_attn_block, preferred_element_t...  60.7 us
    all_gather x1, waiting for transfers between devices, per_device(): lax.all_gather(packed, 'seq', axis=0, tiled=True)  53.4 us
    psum x1, waiting for transfers between devices, per_device(): lax.psum(jnp.dot(act_low, w_down, preferred_element_type=jnp.float32), 'mp')  43 us
  transfers between devices with their start and end apart: 13, of which 9 were waited for; matrix products, arithmetic and copies ran while one was open for 3% of the time, Pallas kernels for 0%

profile of v1, /device:TPU:0, one launch (start us, length us, event | category | flops | bytes accessed | tf_op | source)
XLA Modules:
  0.0 1069.7 jit_solution(6018001746182230373)
XLA Ops:
  8.2 2.0 fusion.101
  14.3 4.9 collective-permute-start
  25.7 53.4 %all-gather.2.cloned.1.call-done = bf16[4096,384]{0,1:T(8,128)(2,1)} async-done(((bf16[512,384]{0,1:T(8,128)(2,1)}), bf16[4096,384]{0,1:T(8,128)(2,1)}) %all-gather.2.cloned.1.call-update) | async-done | bytes 3145744 | tf_op jit(solution)/shard_map/all_gather | solution.py:164
  79.2 4.0 copy.145
  83.1 90.0 %while.26 = (s32[]{:T(128)}, f32[512,3,64]{0,2,1:T(8,128)S(1)}, bf16[4,1024,384]{1,2,0:T(8,128)(2,1)}, s32[512]{0:T(512)S(1)}, s32[4]{0:T(128)S(1)}, /*index=5*/...) while((s32[]{:T(128)}, f32[512,3,64]{0,2,1:T(8,128)S(1)}, ...), condition=%wide.region_6.7_spmd.clone, body=%wide.region_4.6_spmd.clone.sunk | while | flops 421229568 | bytes 9136299 | solution.py:79
  89.6 16.3 %fusion.364 = f32[512,3,64]{0,2,1:T(8,128)S(1)} fusion(bf16[1024,3,64]{0,2,1:T(8,128)(2,1)S(1)} %bitcast.401, f32[512,1024]{0,1:T(8,128)} %compare_convert_fusion.4, bf16[1024,3,64]{0,2,1:T(8,128)(2,1)S(1)} %bitcast.400, bf16[512,3,64]{0,2,1:T(8,128)(2,1)S(1)} %get-tuple-element.668, f32[512,3,64]{0,2,1:T(8,128)S(1)} %get-tuple-element.654, ...), kind=kOutput, calls=%fused_computation.16.clone.1 | convolution fusion | flops 420151296 | bytes 3866625 | tf_op jit(solution)/shard_map/while/body/eval_jaxpr/hbk,khe->bhe/dot_general | solution.py:159
  111.9 16.3 %fusion.364 = f32[512,3,64]{0,2,1:T(8,128)S(1)} fusion(bf16[1024,3,64]{0,2,1:T(8,128)(2,1)S(1)} %bitcast.401, f32[512,1024]{0,1:T(8,128)} %compare_convert_fusion.4, bf16[1024,3,64]{0,2,1:T(8,128)(2,1)S(1)} %bitcast.400, bf16[512,3,64]{0,2,1:T(8,128)(2,1)S(1)} %get-tuple-element.668, f32[512,3,64]{0,2,1:T(8,128)S(1)} %get-tuple-element.654, ...), kind=kOutput, calls=%fused_computation.16.clone.1 | convolution fusion | flops 420151296 | bytes 3866625 | tf_op jit(solution)/shard_map/while/body/eval_jaxpr/hbk,khe->bhe/dot_general | solution.py:159
  134.3 16.3 %fusion.364 = f32[512,3,64]{0,2,1:T(8,128)S(1)} fusion(bf16[1024,3,64]{0,2,1:T(8,128)(2,1)S(1)} %bitcast.401, f32[512,1024]{0,1:T(8,128)} %compare_convert_fusion.4, bf16[1024,3,64]{0,2,1:T(8,128)(2,1)S(1)} %bitcast.400, bf16[512,3,64]{0,2,1:T(8,128)(2,1)S(1)} %get-tuple-element.668, f32[512,3,64]{0,2,1:T(8,128)S(1)} %get-tuple-element.654, ...), kind=kOutput, calls=%fused_computation.16.clone.1 | convolution fusion | flops 420151296 | bytes 3866625 | tf_op jit(solution)/shard_map/while/body/eval_jaxpr/hbk,khe->bhe/dot_general | solution.py:159
  156.6 16.3 %fusion.364 = f32[512,3,64]{0,2,1:T(8,128)S(1)} fusion(bf16[1024,3,64]{0,2,1:T(8,128)(2,1)S(1)} %bitcast.401, f32[512,1024]{0,1:T(8,128)} %compare_convert_fusion.4, bf16[1024,3,64]{0,2,1:T(8,128)(2,1)S(1)} %bitcast.400, bf16[512,3,64]{0,2,1:T(8,128)(2,1)S(1)} %get-tuple-element.668, f32[512,3,64]{0,2,1:T(8,128)S(1)} %get-tuple-element.654, ...), kind=kOutput, calls=%fused_computation.16.clone.1 | convolution fusion | flops 420151296 | bytes 3866625 | tf_op jit(solution)/shard_map/while/body/eval_jaxpr/hbk,khe->bhe/dot_general | solution.py:159
  174.1 6.2 fusion.241
  181.0 1.6 fusion.303
  182.7 41.1 %all-reduce.8.cloned.1.call-done = f32[512,768]{1,0:T(8,128)} async-done(((f32[512,768]{1,0:T(8,128)}), f32[512,768]{1,0:T(8,128)}) %all-reduce.8.cloned.1.call-update) | async-done | bytes 1572880 | tf_op jit(solution)/shard_map/psum | solution.py:181
  223.8 1.9 fusion.290
  226.4 5.1 fusion.87
  232.4 1.9 fusion.304
  234.4 43.0 %all-reduce.10.cloned.1.call-done = f32[512,768]{1,0:T(8,128)} async-done(((f32[512,768]{1,0:T(8,128)}), f32[512,768]{1,0:T(8,128)}) %all-reduce.10.cloned.1.call-update) | async-done | bytes 1572880 | tf_op jit(solution)/shard_map/psum | solution.py:187
  277.4 2.0 fusion.289
  281.9 2.1 fusion.286
  284.0 1.7 fusion.299
  286.6 2.0 fusion.305
  288.9 42.8 %all-reduce.12.cloned.1.call-done = f32[512,768]{1,0:T(8,128)} async-done(((f32[512,768]{1,0:T(8,128)}), f32[512,768]{1,0:T(8,128)}) %all-reduce.12.cloned.1.call-update) | async-done | bytes 1572880 | tf_op jit(solution)/shard_map/psum | solution.py:204
  331.7 3.3 multiply_reduce_fusion
  336.2 3.1 fusion.219
  341.9 18.0 %collective-permute-done.2 = bf16[512,768]{0,1:T(8,128)(2,1)} collective-permute-done((bf16[512,768]{0,1:T(8,128)(2,1)}, bf16[512,768]{0,1:T(8,128)(2,1)}, u32[]{:S(2)}, u32[]{:S(2)}) %collective-permute-start.2) | collective-permute-done | bytes 786464 | tf_op jit(solution)/shard_map/ppermute | solution.py:16
  359.9 10.8 %maximum_select_fusion.2 = bf16[1024,768]{0,1:T(8,128)(2,1)} fusion(bf16[512,768]{0,1:T(8,128)(2,1)} %collective-permute-done.2, bf16[512,192]{0,1:T(8,128)(2,1)S(1)} %bitcast.403, bf16[512,192]{0,1:T(8,128)(2,1)S(1)} %copy-done.22, bf16[512,192]{0,1:T(8,128)(2,1)S(1)} %copy-done.17, bf16[512,192]{0,1:T(8,128)(2,1)S(1)} %copy-done.21, pred[]{:T(512)S(6)} %eq.224), kind=kLoop, calls=%fused_computation.142 | loop fusion | flops 16515072 | bytes 3145729 | tf_op jit(solution)/shard_map/jit(_where)/select_n | solution.py:19
  372.2 33.9 %collective-permute-done.3 = bf16[1024,768]{0,1:T(8,128)(2,1)} collective-permute-done((bf16[1024,768]{0,1:T(8,128)(2,1)}, bf16[1024,768]{0,1:T(8,128)(2,1)}, u32[]{:S(2)}, u32[]{:S(2)}) %collective-permute-start.3) | collective-permute-done | bytes 1572896 | tf_op jit(solution)/shard_map/ppermute | solution.py:16
  406.1 5.2 maximum_select_fusion.1
  411.3 2.4 collective-permute-start.4
  414.4 3.3 convolution_convert_fusion.1
  417.8 3.4 collective-permute-start.5
  422.5 1.8 convolution_convert_fusion
  424.4 2.8 collective-permute-done.6
  428.1 120.2 %collective-permute-done.4 = bf16[2048,768]{0,1:T(8,128)(2,1)} collective-permute-done((bf16[2048,768]{0,1:T(8,128)(2,1)}, bf16[2048,768]{0,1:T(8,128)(2,1)}, u32[]{:S(2)}, u32[]{:S(2)}) %collective-permute-start.4) | collective-permute-done | bytes 3145760 | tf_op jit(solution)/shard_map/ppermute | solution.py:16
  548.3 7.3 maximum_select_fusion
  555.6 3.4 copy.144
  559.0 303.2 %while.27 = (s32[]{:T(128)}, f32[512,3,64]{0,2,1:T(8,128)}, f32[512,3,64]{0,2,1:T(8,128)}, f32[512,3,64]{0,2,1:T(8,128)}, bf16[4,1024,768]{1,2,0:T(8,128)(2,1)},...) while((s32[]{:T(128)}, f32[512,3,64]{0,2,1:T(8,128)}, ...), condition=%wide.region_23.24_spmd.clone, body=%wide.region_21.23_spmd.clone.sunk | while | flops 1486976000 | bytes 64526712 | solution.py:79
  565.2 3.7 fusion.381
  568.9 21.3 %fusion.382 = f32[512,3,64]{0,2,1:T(8,128)} fusion(bf16[1024,3,64]{0,2,1:T(8,128)(2,1)S(1)} %bitcast.393, f32[3,1024,512]{2,1,0:T(8,128)} %fusion.381, f32[1024,512]{1,0:T(8,128)S(1)} %compare_select_fusion.5, bf16[1024,3,64]{0,2,1:T(8,128)(2,1)} %bitcast.398, bf16[512,3,64]{0,2,1:T(8,128)(2,1)} %get-tuple-element.709, ...), kind=kOutput, calls=%fused_computation.66.clone.1 | convolution fusion | flops 431161344 | bytes 10158081 | tf_op jit(solution)/shard_map/while/body/eval_jaxpr/hbk,bhe->khe/dot_general | solution.py:257
  591.3 15.2 %fusion.383 = f32[512,3,64]{0,2,1:T(8,128)S(1)} fusion(bf16[1024,3,64]{0,2,1:T(8,128)(2,1)S(1)} %bitcast.399, f32[3,1024,512]{2,1,0:T(8,128)} %fusion.381, f32[1024,512]{1,0:T(8,128)S(1)} %compare_convert_fusion.5, f32[512,3,64]{0,2,1:T(8,128)S(1)} %copy-done.37, pred[]{:T(512)S(6)} %compare.7), kind=kOutput, calls=%fused_computation.65.clone.1 | convolution fusion | flops 218824704 | bytes 9568257 | tf_op jit(solution)/shard_map/while/body/eval_jaxpr/hbk,bhe->khe/dot_general | solution.py:260
  606.7 3.7 fusion.379
  610.4 21.3 %fusion.380 = f32[512,3,64]{0,2,1:T(8,128)S(1)} fusion(bf16[1024,3,64]{0,2,1:T(8,128)(2,1)S(1)} %bitcast.397, f32[3,1024,512]{2,1,0:T(8,128)} %fusion.379, f32[512,1024]{0,1:T(8,128)S(1)} %compare_select_fusion.4, bf16[512,3,64]{0,2,1:T(8,128)(2,1)} %get-tuple-element.708, f32[512,3,64]{0,2,1:T(8,128)S(1)} %copy-done.40, pred[]{:T(512)S(6)} %compare.7), kind=kOutput, calls=%fused_computation.67.clone.1 | convolution fusion | flops 431161344 | bytes 9764865 | tf_op jit(solution)/shard_map/while/body/eval_jaxpr/hbk,khe->bhe/dot_general | solution.py:251
  638.8 3.7 fusion.381
  642.4 21.5 %fusion.382 = f32[512,3,64]{0,2,1:T(8,128)} fusion(bf16[1024,3,64]{0,2,1:T(8,128)(2,1)S(1)} %bitcast.393, f32[3,1024,512]{2,1,0:T(8,128)} %fusion.381, f32[1024,512]{1,0:T(8,128)S(1)} %compare_select_fusion.5, bf16[1024,3,64]{0,2,1:T(8,128)(2,1)} %bitcast.398, bf16[512,3,64]{0,2,1:T(8,128)(2,1)} %get-tuple-element.709, ...), kind=kOutput, calls=%fused_computation.66.clone.1 | convolution fusion | flops 431161344 | bytes 10158081 | tf_op jit(solution)/shard_map/while/body/eval_jaxpr/hbk,bhe->khe/dot_general | solution.py:257
  665.1 15.2 %fusion.383 = f32[512,3,64]{0,2,1:T(8,128)S(1)} fusion(bf16[1024,3,64]{0,2,1:T(8,128)(2,1)S(1)} %bitcast.399, f32[3,1024,512]{2,1,0:T(8,128)} %fusion.381, f32[1024,512]{1,0:T(8,128)S(1)} %compare_convert_fusion.5, f32[512,3,64]{0,2,1:T(8,128)S(1)} %copy-done.37, pred[]{:T(512)S(6)} %compare.7), kind=kOutput, calls=%fused_computation.65.clone.1 | convolution fusion | flops 218824704 | bytes 9568257 | tf_op jit(solution)/shard_map/while/body/eval_jaxpr/hbk,bhe->khe/dot_general | solution.py:260
  680.5 3.7 fusion.379
  684.2 21.1 %fusion.380 = f32[512,3,64]{0,2,1:T(8,128)S(1)} fusion(bf16[1024,3,64]{0,2,1:T(8,128)(2,1)S(1)} %bitcast.397, f32[3,1024,512]{2,1,0:T(8,128)} %fusion.379, f32[512,1024]{0,1:T(8,128)S(1)} %compare_select_fusion.4, bf16[512,3,64]{0,2,1:T(8,128)(2,1)} %get-tuple-element.708, f32[512,3,64]{0,2,1:T(8,128)S(1)} %copy-done.40, pred[]{:T(512)S(6)} %compare.7), kind=kOutput, calls=%fused_computation.67.clone.1 | convolution fusion | flops 431161344 | bytes 9764865 | tf_op jit(solution)/shard_map/while/body/eval_jaxpr/hbk,khe->bhe/dot_general | solution.py:251
  712.6 3.7 fusion.381
  716.3 21.3 %fusion.382 = f32[512,3,64]{0,2,1:T(8,128)} fusion(bf16[1024,3,64]{0,2,1:T(8,128)(2,1)S(1)} %bitcast.393, f32[3,1024,512]{2,1,0:T(8,128)} %fusion.381, f32[1024,512]{1,0:T(8,128)S(1)} %compare_select_fusion.5, bf16[1024,3,64]{0,2,1:T(8,128)(2,1)} %bitcast.398, bf16[512,3,64]{0,2,1:T(8,128)(2,1)} %get-tuple-element.709, ...), kind=kOutput, calls=%fused_computation.66.clone.1 | convolution fusion | flops 431161344 | bytes 10158081 | tf_op jit(solution)/shard_map/while/body/eval_jaxpr/hbk,bhe->khe/dot_general | solution.py:257
  738.7 15.2 %fusion.383 = f32[512,3,64]{0,2,1:T(8,128)S(1)} fusion(bf16[1024,3,64]{0,2,1:T(8,128)(2,1)S(1)} %bitcast.399, f32[3,1024,512]{2,1,0:T(8,128)} %fusion.381, f32[1024,512]{1,0:T(8,128)S(1)} %compare_convert_fusion.5, f32[512,3,64]{0,2,1:T(8,128)S(1)} %copy-done.37, pred[]{:T(512)S(6)} %compare.7), kind=kOutput, calls=%fused_computation.65.clone.1 | convolution fusion | flops 218824704 | bytes 9568257 | tf_op jit(solution)/shard_map/while/body/eval_jaxpr/hbk,bhe->khe/dot_general | solution.py:260
  754.1 3.7 fusion.379
  757.8 21.3 %fusion.380 = f32[512,3,64]{0,2,1:T(8,128)S(1)} fusion(bf16[1024,3,64]{0,2,1:T(8,128)(2,1)S(1)} %bitcast.397, f32[3,1024,512]{2,1,0:T(8,128)} %fusion.379, f32[512,1024]{0,1:T(8,128)S(1)} %compare_select_fusion.4, bf16[512,3,64]{0,2,1:T(8,128)(2,1)} %get-tuple-element.708, f32[512,3,64]{0,2,1:T(8,128)S(1)} %copy-done.40, pred[]{:T(512)S(6)} %compare.7), kind=kOutput, calls=%fused_computation.67.clone.1 | convolution fusion | flops 431161344 | bytes 9764865 | tf_op jit(solution)/shard_map/while/body/eval_jaxpr/hbk,khe->bhe/dot_general | solution.py:251
  786.2 3.7 fusion.381
  789.9 21.5 %fusion.382 = f32[512,3,64]{0,2,1:T(8,128)} fusion(bf16[1024,3,64]{0,2,1:T(8,128)(2,1)S(1)} %bitcast.393, f32[3,1024,512]{2,1,0:T(8,128)} %fusion.381, f32[1024,512]{1,0:T(8,128)S(1)} %compare_select_fusion.5, bf16[1024,3,64]{0,2,1:T(8,128)(2,1)} %bitcast.398, bf16[512,3,64]{0,2,1:T(8,128)(2,1)} %get-tuple-element.709, ...), kind=kOutput, calls=%fused_computation.66.clone.1 | convolution fusion | flops 431161344 | bytes 10158081 | tf_op jit(solution)/shard_map/while/body/eval_jaxpr/hbk,bhe->khe/dot_general | solution.py:257
  812.5 15.2 %fusion.383 = f32[512,3,64]{0,2,1:T(8,128)S(1)} fusion(bf16[1024,3,64]{0,2,1:T(8,128)(2,1)S(1)} %bitcast.399, f32[3,1024,512]{2,1,0:T(8,128)} %fusion.381, f32[1024,512]{1,0:T(8,128)S(1)} %compare_convert_fusion.5, f32[512,3,64]{0,2,1:T(8,128)S(1)} %copy-done.37, pred[]{:T(512)S(6)} %compare.7), kind=kOutput, calls=%fused_computation.65.clone.1 | convolution fusion | flops 218824704 | bytes 9568257 | tf_op jit(solution)/shard_map/while/body/eval_jaxpr/hbk,bhe->khe/dot_general | solution.py:260
  827.9 3.7 fusion.379
  831.6 21.1 %fusion.380 = f32[512,3,64]{0,2,1:T(8,128)S(1)} fusion(bf16[1024,3,64]{0,2,1:T(8,128)(2,1)S(1)} %bitcast.397, f32[3,1024,512]{2,1,0:T(8,128)} %fusion.379, f32[512,1024]{0,1:T(8,128)S(1)} %compare_select_fusion.4, bf16[512,3,64]{0,2,1:T(8,128)(2,1)} %get-tuple-element.708, f32[512,3,64]{0,2,1:T(8,128)S(1)} %copy-done.40, pred[]{:T(512)S(6)} %compare.7), kind=kOutput, calls=%fused_computation.67.clone.1 | convolution fusion | flops 431161344 | bytes 9764865 | tf_op jit(solution)/shard_map/while/body/eval_jaxpr/hbk,khe->bhe/dot_general | solution.py:251
  864.1 1.6 fusion.115
  866.0 6.2 fusion.242
  872.3 1.7 bitcast_convert_fusion
  893.1 37.1 %all-reduce = (bf16[2,192]{1,0:T(2,128)(2,1)S(1)}, bf16[3,33]{1,0:T(4,128)(2,1)S(1)}, bf16[768]{0:T(1024)(128)(2,1)S(1)}, bf16[768]{0:T(1024)(128)(2,1)S(1)}, bf...) all-reduce(bf16[2,192]{1,0:T(2,128)(2,1)S(1)} %pad_maximum_fusion.4, ...), channel_id=1, replica_groups=mesh['seq'=8,'mp'=4] {'seq'}, use_global_device_ids=true, to_apply=%region_29.30 | all-reduce | flops 5859 | bytes 23436 | tf_op jit(solution)/shard_map/psum | solution.py:291
  935.5 2.2 add_convert_fusion
  937.7 118.2 %all-reduce.16.cloned.1.call-done = (bf16[3,768,192]{1,2,0:T(8,128)(2,1)}, bf16[192,768]{1,0:T(8,128)(2,1)}, bf16[768,768]{1,0:T(8,128)(2,1)}, bf16[768,768]{1,0:T(8,128)(2,1)}) async-done(((bf16[3,768,192]{1,2,0:T(8,128)(2,1)}, bf16[192,768]{1,0:T(8,128)(2,1)}, bf16[768,768]{1,0:T(8,128)(2,1)}, bf16[768,768]{1,0:T(8,128)(2,1)}), (bf16[3,768,192]{1,2,0:T(8,128)(2,1)}, bf16[192,768]{1,0:T(8,128)(2,1)}, ...) | async-done | bytes 3538960 | tf_op jit(solution)/shard_map/psum | solution.py:290
  1055.9 2.9 convert_element_type.398
  1058.8 1.6 convert_element_type.401
  (629 shorter events, 108.6 us)
Async XLA Ops:
  7.2 218.9 %copy-start = (bf16[768,768]{1,0:T(8,128)(2,1)S(1)}, bf16[768,768]{1,0:T(8,128)(2,1)}, u32[]{:S(2)}) copy-start(bf16[768,768]{1,0:T(8,128)(2,1)} %param.29) | copy-start | bytes 3538948
  7.2 72.0 %all-gather.2.cloned.1.call-start = ((), (), s32[]{:S(2)}) async-start(), calls=%async_computation | async-start | bytes 3538944 | tf_op jit(solution)/shard_map/all_gather | solution.py:164
  10.3 14.9 %copy-start.15 = (f32[1,512,192]{1,2,0:T(8,128)}, f32[1,512,192]{1,2,0:T(8,128)S(1)}, u32[]{:S(2)}) copy-start(f32[1,512,192]{1,2,0:T(8,128)S(1)} %get-tuple-element.434) | copy-start | bytes 1179652
  10.4 15.2 %copy-start.16 = (bf16[512,192]{0,1:T(8,128)(2,1)}, bf16[512,192]{0,1:T(8,128)(2,1)S(1)}, u32[]{:S(2)}) copy-start(bf16[512,192]{0,1:T(8,128)(2,1)S(1)} %slice_bitcast_fusion.2) | copy-start | bytes 589828
  11.1 9.3 copy-start.160
  11.2 10.1 copy-start.145
  11.2 14.1 %copy-start.48 = (f32[512,3]{0,1:T(4,128)}, f32[512,3]{0,1:T(4,128)S(1)}, u32[]{:S(2)}) copy-start(f32[512,3]{0,1:T(4,128)S(1)} %get-tuple-element.514) | copy-start | bytes 18436
  11.2 402.5 %copy-start.46 = (f32[512,3]{0,1:T(4,128)}, f32[512,3]{0,1:T(4,128)S(1)}, u32[]{:S(2)}) copy-start(f32[512,3]{0,1:T(4,128)S(1)} %get-tuple-element.515) | copy-start | bytes 18436
  13.4 210.4 %all-reduce.8.cloned.1.call-start = ((), (), s32[]{:S(2)}) async-start(), calls=%async_computation.1 | async-start | bytes 3145728 | tf_op jit(solution)/shard_map/psum | solution.py:181
  14.3 11.2 %collective-permute-start = (bf16[16,192]{0,1:T(8,128)(2,1)S(1)}, bf16[16,192]{0,1:T(8,128)(2,1)S(1)}, u32[]{:S(2)}, u32[]{:S(2)}) collective-permute-start(bf16[16,192]{0,1:T(8,128)(2,1)S(1)} %get-tuple-element.438), channel_id=1, source_target_pairs={{0,4},{4,8},{8,12},{12,16},{16,20},{20,24},{24,28},{1,5},{5,9},{9,... | collective-permute-start | bytes 18440 | tf_op jit(solution)/shard_map/ppermute | solution.py:32
  19.2 6.3 collective-permute-start.1
  23.1 313.0 %copy-start.123 = (f32[512]{0:T(512)}, f32[512]{0:T(512)S(1)}, u32[]{:S(2)}) copy-start(f32[512]{0:T(512)S(1)} %get-tuple-element.423) | copy-start | bytes 6148
  23.7 150.1 %copy-start.128 = (f32[1,192]{1,0:T(1,128)}, f32[1,192]{1,0:T(1,128)S(1)}, u32[]{:S(2)}) copy-start(f32[1,192]{1,0:T(1,128)S(1)} %get-tuple-element.459) | copy-start | bytes 2308
  23.7 150.1 %copy-start.130 = (f32[1,192]{1,0:T(1,128)}, f32[1,192]{1,0:T(1,128)S(1)}, u32[]{:S(2)}) copy-start(f32[1,192]{1,0:T(1,128)S(1)} %get-tuple-element.460) | copy-start | bytes 2308
  23.7 150.1 %copy-start.132 = (f32[1,192]{1,0:T(1,128)}, f32[1,192]{1,0:T(1,128)S(1)}, u32[]{:S(2)}) copy-start(f32[1,192]{1,0:T(1,128)S(1)} %get-tuple-element.461) | copy-start | bytes 2308
  23.7 150.1 %copy-start.134 = (f32[1,192]{1,0:T(1,128)}, f32[1,192]{1,0:T(1,128)S(1)}, u32[]{:S(2)}) copy-start(f32[1,192]{1,0:T(1,128)S(1)} %get-tuple-element.462) | copy-start | bytes 2308
  25.1 148.8 %copy-start.77 = (f32[512]{0:T(512)}, f32[512]{0:T(512)S(1)}, u32[]{:S(2)}) copy-start(f32[512]{0:T(512)S(1)} %get-tuple-element.492) | copy-start | bytes 6148
  25.1 148.8 %copy-start.80 = (f32[512]{0:T(512)}, f32[512]{0:T(512)S(1)}, u32[]{:S(2)}) copy-start(f32[512]{0:T(512)S(1)} %get-tuple-element.493) | copy-start | bytes 6148
  25.1 148.8 %copy-start.83 = (f32[512]{0:T(512)}, f32[512]{0:T(512)S(1)}, u32[]{:S(2)}) copy-start(f32[512]{0:T(512)S(1)} %get-tuple-element.494) | copy-start | bytes 6148
  25.1 148.8 %copy-start.86 = (f32[512]{0:T(512)}, f32[512]{0:T(512)S(1)}, u32[]{:S(2)}) copy-start(f32[512]{0:T(512)S(1)} %get-tuple-element.495) | copy-start | bytes 6148
  25.1 148.8 %copy-start.89 = (f32[512]{0:T(512)}, f32[512]{0:T(512)S(1)}, u32[]{:S(2)}) copy-start(f32[512]{0:T(512)S(1)} %get-tuple-element.496) | copy-start | bytes 6148
  25.1 148.8 %copy-start.92 = (f32[512]{0:T(512)}, f32[512]{0:T(512)S(1)}, u32[]{:S(2)}) copy-start(f32[512]{0:T(512)S(1)} %get-tuple-element.497) | copy-start | bytes 6148
  25.1 148.8 %copy-start.95 = (f32[512]{0:T(512)}, f32[512]{0:T(512)S(1)}, u32[]{:S(2)}) copy-start(f32[512]{0:T(512)S(1)} %get-tuple-element.498) | copy-start | bytes 6148
  25.1 148.8 %copy-start.98 = (f32[512]{0:T(512)}, f32[512]{0:T(512)S(1)}, u32[]{:S(2)}) copy-start(f32[512]{0:T(512)S(1)} %get-tuple-element.499) | copy-start | bytes 6148
  25.1 311.0 %copy-start.125 = (f32[512]{0:T(512)}, f32[512]{0:T(512)S(1)}, u32[]{:S(2)}) copy-start(f32[512]{0:T(512)S(1)} %get-tuple-element.491) | copy-start | bytes 6148
  25.3 148.7 %copy-start.51 = (f32[512]{0:T(512)}, f32[512]{0:T(512)S(1)}, u32[]{:S(2)}) copy-start(f32[512]{0:T(512)S(1)} %get-tuple-element.475) | copy-start | bytes 6148
  25.3 148.7 %copy-start.53 = (f32[512]{0:T(512)}, f32[512]{0:T(512)S(1)}, u32[]{:S(2)}) copy-start(f32[512]{0:T(512)S(1)} %get-tuple-element.476) | copy-start | bytes 6148
  25.3 148.7 %copy-start.55 = (f32[512]{0:T(512)}, f32[512]{0:T(512)S(1)}, u32[]{:S(2)}) copy-start(f32[512]{0:T(512)S(1)} %get-tuple-element.483) | copy-start | bytes 6148
  25.3 148.7 %copy-start.57 = (f32[512]{0:T(512)}, f32[512]{0:T(512)S(1)}, u32[]{:S(2)}) copy-start(f32[512]{0:T(512)S(1)} %get-tuple-element.484) | copy-start | bytes 6148
  25.3 148.7 %copy-start.59 = (f32[512]{0:T(512)}, f32[512]{0:T(512)S(1)}, u32[]{:S(2)}) copy-start(f32[512]{0:T(512)S(1)} %get-tuple-element.485) | copy-start | bytes 6148
  25.3 148.7 %copy-start.62 = (f32[512]{0:T(512)}, f32[512]{0:T(512)S(1)}, u32[]{:S(2)}) copy-start(f32[512]{0:T(512)S(1)} %get-tuple-element.486) | copy-start | bytes 6148
  25.3 148.7 %copy-start.65 = (f32[512]{0:T(512)}, f32[512]{0:T(512)S(1)}, u32[]{:S(2)}) copy-start(f32[512]{0:T(512)S(1)} %get-tuple-element.487) | copy-start | bytes 6148
  25.3 148.7 %copy-start.68 = (f32[512]{0:T(512)}, f32[512]{0:T(512)S(1)}, u32[]{:S(2)}) copy-start(f32[512]{0:T(512)S(1)} %get-tuple-element.488) | copy-start | bytes 6148
  25.3 148.7 %copy-start.71 = (f32[512]{0:T(512)}, f32[512]{0:T(512)S(1)}, u32[]{:S(2)}) copy-start(f32[512]{0:T(512)S(1)} %get-tuple-element.489) | copy-start | bytes 6148
  25.4 148.7 %copy-start.74 = (f32[512]{0:T(512)}, f32[512]{0:T(512)S(1)}, u32[]{:S(2)}) copy-start(f32[512]{0:T(512)S(1)} %get-tuple-element.490) | copy-start | bytes 6148
  25.4 148.7 %copy-start.101 = (f32[512]{0:T(512)}, f32[512]{0:T(512)S(1)}, u32[]{:S(2)}) copy-start(f32[512]{0:T(512)S(1)} %get-tuple-element.477) | copy-start | bytes 6148
  25.4 148.7 %copy-start.104 = (f32[512]{0:T(512)}, f32[512]{0:T(512)S(1)}, u32[]{:S(2)}) copy-start(f32[512]{0:T(512)S(1)} %get-tuple-element.478) | copy-start | bytes 6148
  25.4 148.7 %copy-start.107 = (f32[512]{0:T(512)}, f32[512]{0:T(512)S(1)}, u32[]{:S(2)}) copy-start(f32[512]{0:T(512)S(1)} %get-tuple-element.479) | copy-start | bytes 6148
  25.4 148.7 %copy-start.110 = (f32[512]{0:T(512)}, f32[512]{0:T(512)S(1)}, u32[]{:S(2)}) copy-start(f32[512]{0:T(512)S(1)} %get-tuple-element.480) | copy-start | bytes 6148
  25.4 148.7 %copy-start.113 = (f32[512]{0:T(512)}, f32[512]{0:T(512)S(1)}, u32[]{:S(2)}) copy-start(f32[512]{0:T(512)S(1)} %get-tuple-element.481) | copy-start | bytes 6148
  25.4 148.7 %copy-start.116 = (f32[512]{0:T(512)}, f32[512]{0:T(512)S(1)}, u32[]{:S(2)}) copy-start(f32[512]{0:T(512)S(1)} %get-tuple-element.482) | copy-start | bytes 6148
  25.4 310.7 %copy-start.119 = (f32[512]{0:T(512)}, f32[512]{0:T(512)S(1)}, u32[]{:S(2)}) copy-start(f32[512]{0:T(512)S(1)} %get-tuple-element.473) | copy-start | bytes 6148
  25.4 310.7 %copy-start.121 = (f32[512]{0:T(512)}, f32[512]{0:T(512)S(1)}, u32[]{:S(2)}) copy-start(f32[512]{0:T(512)S(1)} %get-tuple-element.474) | copy-start | bytes 6148
  25.7 310.4 %copy-start.2 = (f32[544,192]{0,1:T(8,128)}, f32[544,192]{0,1:T(8,128)S(1)}, u32[]{:S(2)}) copy-start(f32[544,192]{0,1:T(8,128)S(1)} %maximum_convert_fusion) | copy-start | bytes 1253380
  181.0 42.8 %copy-start.141 = (f32[768]{0:T(1024)S(1)}, f32[768]{0:T(1024)}, u32[]{:S(2)}) copy-start(f32[768]{0:T(1024)} %param.26) | copy-start | bytes 9220
  182.6 94.8 %all-reduce.10.cloned.1.call-start = ((), (), s32[]{:S(2)}) async-start(), calls=%async_computation.2 | async-start | bytes 3145728 | tf_op jit(solution)/shard_map/psum | solution.py:187
  234.3 43.1 %copy-start.142 = (f32[768]{0:T(1024)S(1)}, f32[768]{0:T(1024)}, u32[]{:S(2)}) copy-start(f32[768]{0:T(1024)} %param.32) | copy-start | bytes 9220
  234.4 97.3 %all-reduce.12.cloned.1.call-start = ((), (), s32[]{:S(2)}) async-start(), calls=%async_computation.3 | async-start | bytes 3145728 | tf_op jit(solution)/shard_map/psum | solution.py:204
  288.6 646.9 %all-reduce.14.cloned.1.call-start = ((), (), s32[]{:S(2)}) async-start(), calls=%async_computation.4 | async-start | bytes 1572864 | tf_op jit(solution)/shard_map/psum | solution.py:287
  339.3 87.9 %copy-start.18 = (bf16[512,192]{0,1:T(8,128)(2,1)}, bf16[512,192]{0,1:T(8,128)(2,1)S(1)}, u32[]{:S(2)}) copy-start(bf16[512,192]{0,1:T(8,128)(2,1)S(1)} %get-tuple-element.511) | copy-start | bytes 589828
  340.4 19.5 %collective-permute-start.2 = (bf16[512,768]{0,1:T(8,128)(2,1)}, bf16[512,768]{0,1:T(8,128)(2,1)}, u32[]{:S(2)}, u32[]{:S(2)}) collective-permute-start(bf16[512,768]{0,1:T(8,128)(2,1)} %pad_maximum_fusion), channel_id=1, source_target_pairs={{0,4},{4,0},{8,12},{12,8},{16,20},{20,16},{24,28},{28,24},{1,5},{5... | collective-permute-start | bytes 2359304 | tf_op jit(solution)/shard_map/ppermute | solution.py:16
  370.7 35.4 %collective-permute-start.3 = (bf16[1024,768]{0,1:T(8,128)(2,1)}, bf16[1024,768]{0,1:T(8,128)(2,1)}, u32[]{:S(2)}, u32[]{:S(2)}) collective-permute-start(bf16[1024,768]{0,1:T(8,128)(2,1)} %maximum_select_fusion.2), channel_id=1, source_target_pairs={{0,8},{4,12},{8,0},{12,4},{16,24},{20,28},{24,16},{28,20},{1,9},{5... | collective-permute-start | bytes 4718600 | tf_op jit(solution)/shard_map/ppermute | solution.py:16
  372.2 41.5 %copy-start.14 = (f32[1,512,192]{1,2,0:T(8,128)S(1)}, f32[1,512,192]{1,2,0:T(8,128)}, u32[]{:S(2)}) copy-start(f32[1,512,192]{1,2,0:T(8,128)} %copy-done.13) | copy-start | bytes 1179652
  411.3 137.0 %collective-permute-start.4 = (bf16[2048,768]{0,1:T(8,128)(2,1)}, bf16[2048,768]{0,1:T(8,128)(2,1)}, u32[]{:S(2)}, u32[]{:S(2)}) collective-permute-start(bf16[2048,768]{0,1:T(8,128)(2,1)} %maximum_select_fusion.1), channel_id=1, source_target_pairs={{0,16},{4,20},{8,24},{12,28},{16,0},{20,4},{24,8},{28,12},{1,17},{... | collective-permute-start | bytes 9437192 | tf_op jit(solution)/shard_map/ppermute | solution.py:16
  414.4 8.1 copy-start.30
  417.8 6.5 collective-permute-start.5
  421.2 6.0 collective-permute-start.6
  559.0 303.5 %copy-start.49 = (f32[512,3]{0,1:T(4,128)S(1)}, f32[512,3]{0,1:T(4,128)}, u32[]{:S(2)}) copy-start(f32[512,3]{0,1:T(4,128)} %copy-done.48) | copy-start | bytes 18436
  559.0 305.1 %copy-start.47 = (f32[512,3]{0,1:T(4,128)S(1)}, f32[512,3]{0,1:T(4,128)}, u32[]{:S(2)}) copy-start(f32[512,3]{0,1:T(4,128)} %copy-done.46) | copy-start | bytes 18436
  865.7 9.5 copy-start.32
  874.0 181.9 %all-reduce.16.cloned.1.call-start = ((), (), s32[]{:S(2)}) async-start(), calls=%async_computation.5 | async-start | bytes 7077888 | tf_op jit(solution)/shard_map/psum | solution.py:290
  884.0 8.4 copy-start.147
  884.0 8.8 copy-start.33
  884.0 8.8 copy-start.35
  (130 other events, 414.1 us)
Sparse Core Ops, SparseCore 0:
  13.6 65.5 all-gather.1
  182.7 41.0 all-reduce.7
  234.5 42.8 all-reduce.9
  288.7 42.8 all-reduce.11
  874.1 36.1 all-reduce.13
  915.3 140.5 all-reduce.15
